TPU v7x, 32 devices: a whole 2x2x4 slice. The times are simulated.
32 devices in a mesh: gx: 4 (over x, core), gy: 8 (over z, y).
Axes of the slice: x: 2, y: 2, z: 4, core: 2. Of those that a mesh axis runs over, the one named last changes fastest.
Arguments:
- queries: bfloat16 [256, 2560], P('gx'), may hold values from -8 to 8
- token_key_value: bfloat16 [256, 1024], P('gx'), may hold values from -6 to 6
- group_cached_keys: bfloat16 [4, 32768, 512], P('gx', 'gy'), may hold values from -8 to 8
- group_cached_values: bfloat16 [4, 32768, 512], P('gx', 'gy'), may hold values from -6 to 6
- owners: int32 [4, 32768], P('gx', 'gy'), may hold values from 0 to 63, never falling along the last dimension, each value on 1 to 16384 neighbouring positions
- out_weight: bfloat16 [2560, 2560], P(None, 'gy'), may hold values from -0.125 to 0.125
- residual: bfloat16 [256, 2560], P('gx', 'gy'), may hold values from -6 to 6
- norm_gain: bfloat16 [2560], P('gy'), may hold values from 0.099609375 to 1.8984375
- expert_ids: int32 [256, 6], replicated, may hold values from 0 to 63, all different within a row; in each aligned block of 64 rows (0 to 63, 64 to 127, ...) at most 12 rows name the same one
- gate_logits: float32 [256, 6], replicated, may hold values from -0.5 to 0.5
- w_gate_up: bfloat16 [64, 2560, 3072], P('gx', 'gy'), may hold values from -0.125 to 0.125
- w_down: bfloat16 [64, 1536, 2560], P('gx', None, 'gy'), may hold values from -0.15625 to 0.15625
Outputs:
- layer_out: float32 [256, 2560], P('gx', 'gy')
Inputs may be any that keep to these rules, and one draw needn't show every extreme that they name: `owners`: each request's positions form one run; every request owns at least one position and at most 16384, and some request owns exactly 16384. `expert_ids`: within each group of 64 requests no expert is named by more than 12 requests, a bound that some block reaches.
All inputs are finite; a program needn't handle non-finite values.
Results may differ from a plain program's by a relative error of at most 0.0075.
Values may be sent and summed in bfloat16 or wider, within the bound.
No kernel may reach another device: no remote copies, remote signals or barrier semaphores. Data moves between devices by JAX's collectives and lax.ppermute only.
A program may use at most 192 MiB of HBM per device.

v0:
```python
import jax
import jax.numpy as jnp
from jax import lax
from jax.sharding import PartitionSpec as P

D = 2560
QUERY_HEADS = 20
KEY_VALUE_HEADS = 4
HEAD_SIZE = 128
E = 64
TOPK = 6
CAPS = 12
minimal_score = -1e30
norm_epsilon = 1e-05


def merged(part, axis, combine):
    gathered = jax.tree.map(lambda a: lax.all_gather(a, axis), part)

    def take(source):
        return jax.tree.map(lambda a: lax.dynamic_index_in_dim(a, source, 0, False), gathered)

    return lax.fori_loop(
        1, lax.axis_size(axis), lambda source, state: combine(state, take(source)), take(0)
    )


def merge_partial(earlier_part, later_part):
    max_one, den_one, acc_one = earlier_part
    max_two, den_two, acc_two = later_part
    peak = jnp.maximum(max_one, max_two)
    scale_one = jnp.exp(max_one - peak)
    scale_two = jnp.exp(max_two - peak)
    return (
        peak,
        den_one * scale_one + den_two * scale_two,
        acc_one * scale_one[..., None] + acc_two * scale_two[..., None],
    )


def slot_ranks(flat_ids, num_experts):
    onehot = (flat_ids[..., None] == lax.iota(jnp.int32, num_experts)).astype(jnp.int32)
    earlier = jnp.cumsum(onehot, axis=-2) - onehot
    return jnp.sum(earlier * onehot, axis=-1)


def attend_local(queries, group_cached_keys, group_cached_values, owners):
    request_rows = queries.shape[0]
    query_heads_per_group = QUERY_HEADS // KEY_VALUE_HEADS
    positions = group_cached_keys.shape[0]
    block_length = min(positions, 512)
    block_count = positions // block_length
    key_block_list = group_cached_keys.reshape(
        block_count, block_length, KEY_VALUE_HEADS, HEAD_SIZE
    )
    value_block_list = group_cached_values.reshape(
        block_count, block_length, KEY_VALUE_HEADS, HEAD_SIZE
    )
    owner_blocks = owners.reshape(block_count, block_length)
    scaling = HEAD_SIZE ** (-0.5)
    request_ids = lax.iota(jnp.int32, request_rows)

    def visit_block(state_in, inputs):
        run_max, run_den, run_acc = state_in
        key_block, value_block, owning_block = inputs
        picked_experts = queries[owning_block].reshape(
            block_length, KEY_VALUE_HEADS, query_heads_per_group, HEAD_SIZE
        )
        scores = (
            jnp.einsum(
                "tkgd,tkd->tkg", picked_experts, key_block, preferred_element_type=jnp.float32
            )
            * scaling
        )
        member = owning_block[:, None] == request_ids[None, :]
        block_max = jnp.max(
            jnp.where(member[:, :, None, None], scores[:, None], minimal_score), axis=0
        )
        new_max = jnp.maximum(run_max, block_max)
        prob_block = jnp.exp(scores - new_max[owning_block]).astype(jnp.bfloat16)
        spread = jnp.where(
            member[:, :, None, None], prob_block[:, None], jnp.zeros((), jnp.bfloat16)
        )
        rescale = jnp.exp(run_max - new_max)
        run_den = run_den * rescale + jnp.sum(spread.astype(jnp.float32), axis=0)
        run_acc = run_acc * rescale[..., None] + jnp.einsum(
            "trkg,tkd->rkgd", spread, value_block, preferred_element_type=jnp.float32
        )
        return ((new_max, run_den, run_acc), None)

    initial = (
        jnp.full(
            (request_rows, KEY_VALUE_HEADS, query_heads_per_group), minimal_score, jnp.float32
        ),
        jnp.zeros((request_rows, KEY_VALUE_HEADS, query_heads_per_group), jnp.float32),
        jnp.zeros((request_rows, KEY_VALUE_HEADS, query_heads_per_group, HEAD_SIZE), jnp.float32),
    )
    return lax.scan(visit_block, initial, (key_block_list, value_block_list, owner_blocks))[0]


def expert_block(tokens, w_gate_up, w_down):
    hidden_units = w_down.shape[1]
    gate_up = jnp.einsum("sekd,edf->sekf", tokens, w_gate_up, preferred_element_type=jnp.float32)
    gate_up = lax.psum(gate_up, "gy")
    active = (jax.nn.silu(gate_up[..., :hidden_units]) * gate_up[..., hidden_units:]).astype(
        jnp.bfloat16
    )
    return jnp.einsum("sekf,efd->sekd", active, w_down, preferred_element_type=jnp.float32).astype(
        jnp.bfloat16
    )


def shards(
    queries,
    token_key_value,
    group_cached_keys,
    group_cached_values,
    owners,
    out_weight,
    residual,
    norm_gain,
    expert_ids,
    gate_logits,
    w_gate_up,
    w_down,
):
    request_rows = queries.shape[0]
    query_heads_per_group = QUERY_HEADS // KEY_VALUE_HEADS
    key_value_width = token_key_value.shape[1] // 2
    scaling = HEAD_SIZE ** (-0.5)
    run_max, run_den, run_acc = attend_local(
        queries, group_cached_keys[0], group_cached_values[0], owners[0]
    )
    query_head_rows = queries.reshape(
        request_rows, KEY_VALUE_HEADS, query_heads_per_group, HEAD_SIZE
    )
    appended_keys = token_key_value[:, :key_value_width].reshape(
        request_rows, KEY_VALUE_HEADS, HEAD_SIZE
    )
    appended_values = token_key_value[:, key_value_width:]
    own_score = (
        jnp.einsum(
            "rkgd,rkd->rkg", query_head_rows, appended_keys, preferred_element_type=jnp.float32
        )
        * scaling
    )
    run_max, run_den, run_acc = merged((run_max, run_den, run_acc), "gy", merge_partial)
    peak = jnp.maximum(run_max, own_score)
    rescale = jnp.exp(run_max - peak)
    own_prob = lax.optimization_barrier(jnp.exp(own_score - peak).astype(jnp.bfloat16)).astype(
        jnp.float32
    )
    denominator = run_den * rescale + own_prob
    incoming_values = appended_values.astype(jnp.float32).reshape(
        request_rows, KEY_VALUE_HEADS, 1, HEAD_SIZE
    )
    numerator = run_acc * rescale[..., None] + own_prob[..., None] * incoming_values
    attention = (
        (numerator / denominator[..., None])
        .astype(jnp.bfloat16)
        .reshape(request_rows, QUERY_HEADS * HEAD_SIZE)
    )
    projected = jnp.dot(attention, out_weight, preferred_element_type=jnp.float32)
    hidden = (residual.astype(jnp.float32) + projected).astype(jnp.bfloat16)
    hidden_f = hidden.astype(jnp.float32)
    squares = lax.psum(jnp.sum(hidden_f * hidden_f, axis=1), "gy")
    inv_rms = lax.rsqrt(squares / D + norm_epsilon)
    normed = (hidden_f * inv_rms[:, None] * norm_gain.astype(jnp.float32)[None, :]).astype(
        jnp.bfloat16
    )
    mixing = jax.nn.softmax(gate_logits, axis=-1)
    num_gx = lax.axis_size("gx")
    group_index = lax.axis_index("gx")
    per_row = w_gate_up.shape[0]
    columns_here = normed.shape[1]
    my_ids = lax.dynamic_slice_in_dim(
        expert_ids, group_index * request_rows, request_rows, 0
    ).reshape(-1)
    my_mix = lax.dynamic_slice_in_dim(mixing, group_index * request_rows, request_rows, 0)
    places = my_ids * CAPS + slot_ranks(my_ids, E)
    outgoing = (
        jnp.zeros((E * CAPS, columns_here), jnp.bfloat16)
        .at[places]
        .set(jnp.repeat(normed, TOPK, axis=0))
    )
    returned = lax.all_to_all(
        expert_block(
            lax.all_to_all(
                outgoing.reshape(num_gx, per_row, CAPS, columns_here),
                "gx",
                split_axis=0,
                concat_axis=0,
                tiled=True,
            ),
            w_gate_up,
            w_down,
        ),
        "gx",
        split_axis=0,
        concat_axis=0,
        tiled=True,
    )
    picked = (
        returned.reshape(E * CAPS, columns_here)[places]
        .astype(jnp.float32)
        .reshape(request_rows, TOPK, columns_here)
    )
    routed = jnp.sum(my_mix[..., None] * picked, axis=1)
    return hidden_f + routed


def solution(mesh):
    placed = (
        P("gx", None),
        P("gx", None),
        P("gx", "gy", None),
        P("gx", "gy", None),
        P("gx", "gy"),
        P(None, "gy"),
        P("gx", "gy"),
        P("gy"),
        P(),
        P(),
        P("gx", "gy", None),
        P("gx", None, "gy"),
    )
    return jax.shard_map(
        shards, mesh=mesh, in_specs=placed, out_specs=P("gx", "gy"), check_vma=False
    )
```

profile of v0, /device:TPU:0, one launch (start us, length us, event | category | flops | bytes accessed | tf_op | source)
XLA Modules:
  0.0 817.4 jit_solution(4890092526414652480)
XLA Ops:
  6.5 7.0 reshape.208
  13.6 7.0 reshape_squeeze.10
  22.4 178.0 %while.35 = (s32[]{:T(128)}, f32[64,4,5]{2,1,0:T(4,128)S(1)}, f32[64,4,5]{2,1,0:T(4,128)S(1)}, f32[64,4,5,128]{3,0,2,1:T(8,128)}, s32[8,512]{1,0:T(8,128)}, /*in...) while((s32[]{:T(128)}, f32[64,4,5]{2,1,0:T(4,128)S(1)}, ...), condition=%wide.region_3.4_spmd.clone, body=%wide.region_0.3_spmd.clone.sunk | while | flops 176462592 | bytes 21555320 | solution.py:98
  23.1 3.6 gather_fusion
  26.7 4.5 copy.169
  31.2 2.1 bitcast_convert_fusion.2
  34.9 2.3 multiply_reduce_fusion.4
  44.4 3.6 gather_fusion
  48.0 4.5 copy.169
  52.5 2.1 bitcast_convert_fusion.2
  56.2 2.3 multiply_reduce_fusion.4
  63.6 2.4 fusion.70
  66.8 3.6 gather_fusion
  70.4 4.5 copy.169
  78.6 2.3 multiply_reduce_fusion.4
  86.0 2.4 fusion.70
  89.2 3.6 gather_fusion
  92.8 4.5 copy.169
  101.0 2.3 multiply_reduce_fusion.4
  108.4 2.4 fusion.70
  111.6 3.6 gather_fusion
  115.2 4.5 copy.169
  123.4 2.3 multiply_reduce_fusion.4
  130.8 2.4 fusion.70
  134.0 3.6 gather_fusion
  137.6 4.5 copy.169
  145.8 2.3 multiply_reduce_fusion.4
  153.2 2.4 fusion.70
  156.4 3.6 gather_fusion
  160.0 4.5 copy.169
  168.1 2.3 multiply_reduce_fusion.4
  175.6 2.4 fusion.70
  178.8 3.6 gather_fusion
  182.4 4.5 copy.169
  190.5 2.3 multiply_reduce_fusion.4
  198.0 2.4 fusion.70
  202.2 38.6 %all-gather = f32[512,4,5]{2,1,0:T(4,128)S(1)} all-gather(f32[64,4,5]{2,1,0:T(4,128)S(1)} %get-tuple-element.232), channel_id=2, replica_groups=mesh['gx'=4,'gy'=8] {'gy'}, dimensions={0}, use_global_device_ids=true | all-gather | bytes 46080 | tf_op jit(solution)/shard_map/all_gather | solution.py:18
  240.9 35.2 %all-gather.1 = f32[512,4,5]{2,1,0:T(4,128)S(1)} all-gather(f32[64,4,5]{2,1,0:T(4,128)S(1)} %get-tuple-element.233), channel_id=3, replica_groups=mesh['gx'=4,'gy'=8] {'gy'}, dimensions={0}, use_global_device_ids=true | all-gather | bytes 46080 | tf_op jit(solution)/shard_map/all_gather | solution.py:18
  282.6 27.2 %all-gather.5.cloned.1.call-done = f32[512,4,5,128]{3,0,2,1:T(8,128)} async-done(((f32[64,4,5,128]{3,0,2,1:T(8,128)}), f32[512,4,5,128]{3,0,2,1:T(8,128)}) %all-gather.5.cloned.1.call-update) | async-done | bytes 5242896 | tf_op jit(solution)/shard_map/all_gather | solution.py:18
  311.4 20.6 %while.34 = (s32[]{:T(128)}, f32[64,4,5]{0,1,2:T(4,128)S(1)}, f32[64,4,5]{0,1,2:T(4,128)S(1)}, f32[64,4,5,128]{3,2,1,0:T(8,128)S(1)}, f32[8,64,4,5]{1,2,3,0:T(4,...) while((s32[]{:T(128)}, f32[64,4,5]{0,1,2:T(4,128)S(1)}, ...), condition=%wide.region_5.6_spmd, body=%wide.region_4.5_spmd.sunk | while | flops 499205 | bytes 3348631 | solution.py:23
  336.7 19.3 %psum.14 = f32[64]{0:T(128)S(1)} all-reduce(f32[64]{0:T(128)S(1)} %get-tuple-element.365), channel_id=1, replica_groups=mesh['gx'=4,'gy'=8] {'gy'}, use_global_device_ids=true, to_apply=%region_12.13 | all-reduce | flops 64 | bytes 512 | tf_op jit(solution)/shard_map/psum | solution.py:166
  358.7 12.1 %all_to_all.10 = bf16[4,16,12,320]{3,1,2,0:T(8,128)(2,1)S(1)} all-to-all(bf16[4,16,12,320]{3,1,2,0:T(8,128)(2,1)S(1)} %copy.108), channel_id=1, replica_groups=mesh['gx'=4,'gy'=8] {'gx'}, dimensions={0} | all-to-all | bytes 983040 | tf_op jit(solution)/shard_map/all_to_all | solution.py:188
  370.8 16.6 %fusion.23 = f32[4,16,12,3072]{3,2,0,1:T(8,128)} fusion(bf16[16,320,3072]{2,1,0:T(8,128)(2,1)} %param.26, bf16[4,16,12,320]{3,1,2,0:T(8,128)(2,1)S(1)} %all_to_all.10), kind=kOutput, calls=%fused_computation.44 | convolution fusion | flops 1509949440 | bytes 41385984 | tf_op jit(solution)/shard_map/sekd,edf->sekf/dot_general | solution.py:103
  388.2 393.0 %all-reduce.2.cloned.1.call-done = f32[4,16,12,3072]{3,2,0,1:T(8,128)} async-done(((f32[4,16,12,3072]{3,2,0,1:T(8,128)}), f32[4,16,12,3072]{3,2,0,1:T(8,128)}) %all-reduce.2.cloned.1.call-update) | async-done | bytes 9437200 | tf_op jit(solution)/shard_map/psum | solution.py:104
  781.2 11.6 %fusion.34 = bf16[4,16,12,320]{3,2,0,1:T(8,128)(2,1)S(1)} fusion(bf16[16,1536,320]{1,2,0:T(8,128)(2,1)} %param.27, f32[4,16,12,3072]{3,2,0,1:T(8,128)} %all-reduce.2.cloned.1.call-done), kind=kOutput, calls=%fused_computation.49 | convolution fusion | flops 762298368 | bytes 25657344 | tf_op jit(solution)/shard_map/sekf,efd->sekd/dot_general | solution.py:108
  793.9 3.5 all-to-all-start.1
  797.7 9.2 %all-to-all-done.1 = bf16[4,16,12,320]{3,1,2,0:T(8,128)(2,1)S(1)} async-done(((bf16[4,16,12,320]{3,1,2,0:T(8,128)(2,1)}), bf16[4,16,12,320]{3,1,2,0:T(8,128)(2,1)S(1)}, u32[]{:S(2)}, u32[]{:S(2)}) %all-to-all-start.1) | async-done | bytes 491552 | tf_op jit(solution)/shard_map/all_to_all | solution.py:186
  807.4 2.1 gather_fusion.2
  (276 shorter events, 115.5 us)
Async XLA Ops:
  6.5 329.4 %copy-start = (bf16[2560,320]{0,1:T(8,128)(2,1)S(1)}, bf16[2560,320]{0,1:T(8,128)(2,1)}, u32[]{:S(2)}) copy-start(bf16[2560,320]{0,1:T(8,128)(2,1)} %param.21) | copy-start | bytes 4915204
  6.5 303.3 %all-gather.5.cloned.1.call-start = ((), (), s32[]{:S(2)}) async-start(), calls=%async_computation.3 | async-start | bytes 5898240 | tf_op jit(solution)/shard_map/all_gather | solution.py:18
  13.6 7.5 copy-start.6
  13.6 8.8 %copy-start.1 = (bf16[64,2560]{1,0:T(8,128)(2,1)S(1)}, bf16[64,2560]{1,0:T(8,128)(2,1)}, u32[]{:S(2)}) copy-start(bf16[64,2560]{1,0:T(8,128)(2,1)} %param.16) | copy-start | bytes 983044
  22.4 179.4 %copy-start.7 = (s32[256,6]{0,1:T(8,128)S(1)}, s32[256,6]{0,1:T(8,128)}, u32[]{:S(2)}) copy-start(s32[256,6]{0,1:T(8,128)} %param.24) | copy-start | bytes 18436
  200.4 78.9 %copy-start.3 = (bf16[64,1024]{1,0:T(8,128)(2,1)S(1)}, bf16[64,1024]{1,0:T(8,128)(2,1)}, u32[]{:S(2)}) copy-start(bf16[64,1024]{1,0:T(8,128)(2,1)} %param.17) | copy-start | bytes 393220
  200.5 80.5 %copy-start.8 = (bf16[320]{0:T(512)(128)(2,1)S(1)}, bf16[320]{0:T(512)(128)(2,1)}, u32[]{:S(2)}) copy-start(bf16[320]{0:T(512)(128)(2,1)} %param.23) | copy-start | bytes 1924
  200.5 580.7 %all-reduce.2.cloned.1.call-start = ((), (), s32[]{:S(2)}) async-start(), calls=%async_computation.2 | async-start | bytes 25165824 | tf_op jit(solution)/shard_map/psum | solution.py:104
  276.2 1.0 copy-start.2
  311.4 24.6 %copy-start.4 = (bf16[64,320]{1,0:T(8,128)(2,1)S(1)}, bf16[64,320]{1,0:T(8,128)(2,1)}, u32[]{:S(2)}) copy-start(bf16[64,320]{1,0:T(8,128)(2,1)} %param.22) | copy-start | bytes 122884
  387.4 0.7 copy-start.5
  793.9 13.0 %all-to-all-start.1 = ((bf16[4,16,12,320]{3,1,2,0:T(8,128)(2,1)}), bf16[4,16,12,320]{3,1,2,0:T(8,128)(2,1)S(1)}, u32[]{:S(2)}, u32[]{:S(2)}) async-start(bf16[4,16,12,320]{3,1,2,0:T(8,128)(2,1)} %copy.110), calls=%async_computation.1 | async-start | bytes 1179648 | tf_op jit(solution)/shard_map/all_to_all | solution.py:186
Sparse Core Ops, SparseCore 0:
  200.6 109.1 all-gather.4
  387.6 393.5 all-reduce.1
where the time goes:
time: 821 us; the launch traced here: 817 us
  waiting for transfers between devices  429 us (52%)
  local copies, waits for them, and re-layouts  151 us (18%)
  blocking collectives  105 us (13%)
  other arithmetic  64.6 us (8%)
  matrix products  48.9 us (6%)
  between operations  13.7 us (2%)
    psum x1, waiting for transfers between devices, expert_block(): gate_up = lax.psum(gate_up, 'gy')  393 us
    all_gather x2, blocking collectives, merged(): gathered = jax.tree.map(lambda a: lax.all_gather(a, axis), part)  73.9 us
    while x24, local copies, waits for them, and re-layouts  48.4 us
    while x16, other arithmetic  35.7 us
    gather x8, local copies, waits for them, and re-layouts, visit_block(): queries[owning_block]  28.5 us
    all_gather x1, waiting for transfers between devices, merged(): gathered = jax.tree.map(lambda a: lax.all_gather(a, axis), part)  27.2 us
    gather x16, local copies, waits for them, and re-layouts, visit_block(): prob_block = jnp.exp(scores - new_max[owning_block]).astype(jnp.bfloat16)  19.4 us
    psum x1, blocking collectives, shards(): squares = lax.psum(jnp.sum(hidden_f * hidden_f, axis=1), 'gy')  19.3 us
  transfers between devices with their start and end apart: 3, of which 3 were waited for; matrix products, arithmetic and copies ran while one was open for 1% of the time, Pallas kernels for 0%

commit v1 on v0

--- a/solution.py
+++ b/solution.py
@@ -12,6 +12,22 @@
 CAPS = 12
 minimal_score = -1e30
 norm_epsilon = 1e-05
+
+
+def pairwise_exchange(value, axis, split, join):
+    ways, here = (lax.axis_size(axis), lax.axis_index(axis))
+    width = value.shape[split] // ways
+    lengths = list(value.shape)
+    lengths[split] = width
+    height = lengths[join]
+    lengths[join] = height * ways
+    full = jnp.zeros(lengths, value.dtype)
+    for mask in range(ways):
+        part = lax.dynamic_slice_in_dim(value, (here ^ mask) * width, width, axis=split)
+        if mask:
+            part = lax.ppermute(part, axis, [(d, d ^ mask) for d in range(ways)])
+        full = lax.dynamic_update_slice_in_dim(full, part, (here ^ mask) * height, axis=join)
+    return full
 
 
 def merged(part, axis, combine):
@@ -183,7 +199,7 @@
         .at[places]
         .set(jnp.repeat(normed, TOPK, axis=0))
     )
-    returned = lax.all_to_all(
+    returned = pairwise_exchange(
         expert_block(
             lax.all_to_all(
                 outgoing.reshape(num_gx, per_row, CAPS, columns_here),
@@ -196,9 +212,8 @@
             w_down,
         ),
         "gx",
-        split_axis=0,
-        concat_axis=0,
-        tiled=True,
+        0,
+        0,
     )
     picked = (
         returned.reshape(E * CAPS, columns_here)[places]

time: 821 us -> 819 us (level)
    all_to_all x1 -> x0, waiting for transfers between devices: 9.22 us -> none  [shards(): lax.all_to_all(expert_block(lax.all_to_all(outgoing.reshape(num_gx, per_r...]
  transfers between devices with their start and end apart: 3 -> 5, of which waited for: 3 -> 4; matrix products, arithmetic and copies ran while one was open for 1% -> 1% of each run, Pallas kernels for 0% -> 0%
where the time goes in v1:
time: 819 us; the launch traced here: 815 us
  waiting for transfers between devices  428 us (52%)
  local copies, waits for them, and re-layouts  152 us (19%)
  blocking collectives  105 us (13%)
  other arithmetic  64.6 us (8%)
  matrix products  48.9 us (6%)
  between operations  13.8 us (2%)
    psum x1, waiting for transfers between devices, expert_block(): gate_up = lax.psum(gate_up, 'gy')  393 us
    all_gather x2, blocking collectives, merged(): gathered = jax.tree.map(lambda a: lax.all_gather(a, axis), part)  73.9 us
    while x24, local copies, waits for them, and re-layouts  48.4 us
    while x16, other arithmetic  35.7 us
    gather x8, local copies, waits for them, and re-layouts, visit_block(): queries[owning_block]  28.5 us
    all_gather x1, waiting for transfers between devices, merged(): gathered = jax.tree.map(lambda a: lax.all_gather(a, axis), part)  27.2 us
    gather x16, local copies, waits for them, and re-layouts, visit_block(): prob_block = jnp.exp(scores - new_max[owning_block]).astype(jnp.bfloat16)  19.4 us
    psum x1, blocking collectives, shards(): squares = lax.psum(jnp.sum(hidden_f * hidden_f, axis=1), 'gy')  19.3 us
  transfers between devices with their start and end apart: 5, of which 4 were waited for; matrix products, arithmetic and copies ran while one was open for 1% of the time, Pallas kernels for 0%

profile of v1, /device:TPU:0, one launch (start us, length us, event | category | flops | bytes accessed | tf_op | source)
XLA Modules:
  0.0 815.4 jit_solution(974354665612398548)
XLA Ops:
  6.5 7.0 reshape.212
  13.6 7.0 reshape_squeeze.10
  22.4 178.0 %while.35 = (s32[]{:T(128)}, f32[64,4,5]{2,1,0:T(4,128)S(1)}, f32[64,4,5]{2,1,0:T(4,128)S(1)}, f32[64,4,5,128]{3,0,2,1:T(8,128)}, s32[8,512]{1,0:T(8,128)}, /*in...) while((s32[]{:T(128)}, f32[64,4,5]{2,1,0:T(4,128)S(1)}, ...), condition=%wide.region_3.4_spmd.clone, body=%wide.region_0.3_spmd.clone.sunk | while | flops 176462592 | bytes 21555320 | solution.py:114
  23.1 3.6 gather_fusion
  26.7 4.5 copy.164
  31.2 2.1 bitcast_convert_fusion.2
  34.9 2.3 multiply_reduce_fusion.4
  44.4 3.6 gather_fusion
  48.0 4.5 copy.164
  52.5 2.1 bitcast_convert_fusion.2
  56.2 2.3 multiply_reduce_fusion.4
  63.6 2.4 fusion.65
  66.8 3.6 gather_fusion
  70.4 4.5 copy.164
  78.6 2.3 multiply_reduce_fusion.4
  86.0 2.4 fusion.65
  89.2 3.6 gather_fusion
  92.8 4.5 copy.164
  101.0 2.3 multiply_reduce_fusion.4
  108.4 2.4 fusion.65
  111.6 3.6 gather_fusion
  115.2 4.5 copy.164
  123.4 2.3 multiply_reduce_fusion.4
  130.8 2.4 fusion.65
  134.0 3.6 gather_fusion
  137.6 4.5 copy.164
  145.8 2.3 multiply_reduce_fusion.4
  153.2 2.4 fusion.65
  156.4 3.6 gather_fusion
  160.0 4.5 copy.164
  168.1 2.3 multiply_reduce_fusion.4
  175.6 2.4 fusion.65
  178.8 3.6 gather_fusion
  182.4 4.5 copy.164
  190.5 2.3 multiply_reduce_fusion.4
  198.0 2.4 fusion.65
  202.2 38.6 %all-gather = f32[512,4,5]{2,1,0:T(4,128)S(1)} all-gather(f32[64,4,5]{2,1,0:T(4,128)S(1)} %get-tuple-element.232), channel_id=2, replica_groups=mesh['gx'=4,'gy'=8] {'gy'}, dimensions={0}, use_global_device_ids=true | all-gather | bytes 46080 | tf_op jit(solution)/shard_map/all_gather | solution.py:34
  240.9 35.2 %all-gather.1 = f32[512,4,5]{2,1,0:T(4,128)S(1)} all-gather(f32[64,4,5]{2,1,0:T(4,128)S(1)} %get-tuple-element.233), channel_id=3, replica_groups=mesh['gx'=4,'gy'=8] {'gy'}, dimensions={0}, use_global_device_ids=true | all-gather | bytes 46080 | tf_op jit(solution)/shard_map/all_gather | solution.py:34
  282.6 27.2 %all-gather.5.cloned.1.call-done = f32[512,4,5,128]{3,0,2,1:T(8,128)} async-done(((f32[64,4,5,128]{3,0,2,1:T(8,128)}), f32[512,4,5,128]{3,0,2,1:T(8,128)}) %all-gather.5.cloned.1.call-update) | async-done | bytes 5242896 | tf_op jit(solution)/shard_map/all_gather | solution.py:34
  311.4 20.6 %while.34 = (s32[]{:T(128)}, f32[64,4,5]{0,1,2:T(4,128)S(1)}, f32[64,4,5]{0,1,2:T(4,128)S(1)}, f32[64,4,5,128]{3,2,1,0:T(8,128)S(1)}, f32[8,64,4,5]{1,2,3,0:T(4,...) while((s32[]{:T(128)}, f32[64,4,5]{0,1,2:T(4,128)S(1)}, ...), condition=%wide.region_5.6_spmd, body=%wide.region_4.5_spmd.sunk | while | flops 499205 | bytes 3348631 | solution.py:39
  336.7 19.3 %psum.14 = f32[64]{0:T(128)S(1)} all-reduce(f32[64]{0:T(128)S(1)} %get-tuple-element.368), channel_id=1, replica_groups=mesh['gx'=4,'gy'=8] {'gy'}, use_global_device_ids=true, to_apply=%region_12.13 | all-reduce | flops 64 | bytes 512 | tf_op jit(solution)/shard_map/psum | solution.py:182
  358.7 12.1 %all_to_all.5 = bf16[4,16,12,320]{3,1,2,0:T(8,128)(2,1)S(1)} all-to-all(bf16[4,16,12,320]{3,1,2,0:T(8,128)(2,1)S(1)} %copy.105), channel_id=1, replica_groups=mesh['gx'=4,'gy'=8] {'gx'}, dimensions={0} | all-to-all | bytes 983040 | tf_op jit(solution)/shard_map/all_to_all | solution.py:204
  370.8 16.6 %fusion.23 = f32[4,16,12,3072]{3,2,0,1:T(8,128)} fusion(bf16[16,320,3072]{2,1,0:T(8,128)(2,1)} %param.26, bf16[4,16,12,320]{3,1,2,0:T(8,128)(2,1)S(1)} %all_to_all.5), kind=kOutput, calls=%fused_computation.44 | convolution fusion | flops 1509949440 | bytes 41385984 | tf_op jit(solution)/shard_map/sekd,edf->sekf/dot_general | solution.py:119
  388.3 392.8 %all-reduce.2.cloned.1.call-done = f32[4,16,12,3072]{3,2,0,1:T(8,128)} async-done(((f32[4,16,12,3072]{3,2,0,1:T(8,128)}), f32[4,16,12,3072]{3,2,0,1:T(8,128)}) %all-reduce.2.cloned.1.call-update) | async-done | bytes 9437200 | tf_op jit(solution)/shard_map/psum | solution.py:120
  781.2 11.6 %fusion.29 = bf16[16,4,12,320]{3,2,1,0:T(8,128)(2,1)S(1)} fusion(bf16[16,1536,320]{1,2,0:T(8,128)(2,1)} %param.27, f32[4,16,12,3072]{3,2,0,1:T(8,128)} %all-reduce.2.cloned.1.call-done), kind=kOutput, calls=%fused_computation.48 | convolution fusion | flops 762298368 | bytes 25657344 | tf_op jit(solution)/shard_map/sekf,efd->sekd/dot_general | solution.py:124
  796.9 4.8 collective-permute-done.1
  801.7 3.4 collective-permute-done.2
  805.4 2.1 gather_fusion.2
  (286 shorter events, 118.2 us)
Async XLA Ops:
  6.5 329.4 %copy-start = (bf16[2560,320]{0,1:T(8,128)(2,1)S(1)}, bf16[2560,320]{0,1:T(8,128)(2,1)}, u32[]{:S(2)}) copy-start(bf16[2560,320]{0,1:T(8,128)(2,1)} %param.21) | copy-start | bytes 4915204
  6.5 303.3 %all-gather.5.cloned.1.call-start = ((), (), s32[]{:S(2)}) async-start(), calls=%async_computation.2 | async-start | bytes 5898240 | tf_op jit(solution)/shard_map/all_gather | solution.py:34
  13.6 7.5 copy-start.7
  13.6 8.8 %copy-start.1 = (bf16[64,2560]{1,0:T(8,128)(2,1)S(1)}, bf16[64,2560]{1,0:T(8,128)(2,1)}, u32[]{:S(2)}) copy-start(bf16[64,2560]{1,0:T(8,128)(2,1)} %param.16) | copy-start | bytes 983044
  22.4 179.4 %copy-start.8 = (s32[256,6]{0,1:T(8,128)S(1)}, s32[256,6]{0,1:T(8,128)}, u32[]{:S(2)}) copy-start(s32[256,6]{0,1:T(8,128)} %param.24) | copy-start | bytes 18436
  200.4 78.9 %copy-start.4 = (bf16[64,1024]{1,0:T(8,128)(2,1)S(1)}, bf16[64,1024]{1,0:T(8,128)(2,1)}, u32[]{:S(2)}) copy-start(bf16[64,1024]{1,0:T(8,128)(2,1)} %param.17) | copy-start | bytes 393220
  200.5 80.5 %copy-start.9 = (bf16[320]{0:T(512)(128)(2,1)S(1)}, bf16[320]{0:T(512)(128)(2,1)}, u32[]{:S(2)}) copy-start(bf16[320]{0:T(512)(128)(2,1)} %param.23) | copy-start | bytes 1924
  200.5 580.7 %all-reduce.2.cloned.1.call-start = ((), (), s32[]{:S(2)}) async-start(), calls=%async_computation.1 | async-start | bytes 25165824 | tf_op jit(solution)/shard_map/psum | solution.py:120
  276.2 1.0 copy-start.2
  311.4 24.6 %copy-start.5 = (bf16[64,320]{1,0:T(8,128)(2,1)S(1)}, bf16[64,320]{1,0:T(8,128)(2,1)}, u32[]{:S(2)}) copy-start(bf16[64,320]{1,0:T(8,128)(2,1)} %param.22) | copy-start | bytes 122884
  387.4 0.7 copy-start.6
  792.8 0.9 copy-start.3
  793.7 3.1 collective-permute-start
  793.9 7.7 collective-permute-start.1
  795.4 9.6 %collective-permute-start.2 = (bf16[1,16,12,320]{3,2,1,0:T(8,128)(2,1)S(1)}, bf16[1,16,12,320]{3,2,1,0:T(8,128)(2,1)S(1)}, u32[]{:S(2)}, u32[]{:S(2)}) collective-permute-start(bf16[1,16,12,320]{3,2,1,0:T(8,128)(2,1)S(1)} %get-tuple-element.363), channel_id=1, source_target_pairs={{0,24},{8,16},{16,8},{24,0},{1,25},{9,17},{17,9},{25,1},{2,26},{10... | collective-permute-start | bytes 368648 | tf_op jit(solution)/shard_map/ppermute | solution.py:28
Sparse Core Ops, SparseCore 0:
  200.6 109.1 all-gather.4
  387.6 393.5 all-reduce.1
